TPU v7x, 32 devices: a whole 2x2x4 slice. The times are simulated.
32 devices in a mesh: prow: 4 (over y, core), pcol: 8 (over z, x).
Axes of the slice: x: 2, y: 2, z: 4, core: 2. Of those that a mesh axis runs over, the one named last changes fastest.
Arguments:
- right_side: float32 [8, 256, 128], P(None, 'prow'), may hold values from -6 to 6
- lower_prev: float32 [8, 256, 129024], P(None, 'prow', 'pcol'), may hold values from -0.015625 to 0.015625
- solved_prev: float32 [129024, 128], P('pcol'), may hold values from -6 to 6
- lower_window: float32 [8, 256, 2048], P(None, 'prow', 'pcol'), may hold values from -0.1875 to 0.1875
- inverse_diag: float32 [8, 256, 256], P(None, 'prow'), may hold values from -0.25 to 1.4, as said below
Outputs:
- solution: float32 [8, 256, 128], P(None, 'prow')
Inputs may be any that keep to these rules, and one draw needn't show every extreme that they name: `inverse_diag`: each block is lower triangular: zero above its diagonal, with diagonal entries of 0.7 to 1.4.
All inputs are finite; a program needn't handle non-finite values.
Results may differ from a plain program's by a relative error of at most 0.00011.
Values sent between devices are 32-bit elements; how exact they have to be, the bound alone decides.
No kernel may reach another device: no remote copies, remote signals or barrier semaphores. Data moves between devices by JAX's collectives and lax.ppermute only.
A program may use at most 128 MiB of HBM per device.

v0:
```python
import jax
import jax.numpy as jnp
from jax import lax
from jax.sharding import PartitionSpec as P


def local(right_side, lower_prev, solved_prev, lower_window, inverse_diag):
    highest = lax.Precision.HIGHEST
    blocks = right_side.shape[0]
    local_rows = right_side.shape[1]
    columns = right_side.shape[2]
    block_rows = inverse_diag.shape[2]
    row_start = lax.axis_index("prow") * local_rows
    solved = jnp.zeros((blocks * block_rows, columns), jnp.float32)
    pieces = []
    full_inverse = lax.all_gather(inverse_diag, "prow", axis=1, tiled=True)
    full_window = lax.all_gather(lower_window, "pcol", axis=2, tiled=True)
    for row_block in range(blocks):
        window_term = jnp.dot(
            full_window[row_block], solved, precision=highest, preferred_element_type=jnp.float32
        )
        earlier_part = jnp.dot(
            lower_prev[row_block],
            solved_prev,
            precision=highest,
            preferred_element_type=jnp.float32,
        )
        earlier_here = lax.psum(earlier_part, "pcol")
        local_residual = right_side[row_block] - (earlier_here + window_term)
        residual = lax.all_gather(local_residual, "prow", axis=0, tiled=True)
        whole_rows = jnp.dot(
            full_inverse[row_block], residual, precision=highest, preferred_element_type=jnp.float32
        )
        pieces.append(lax.dynamic_slice_in_dim(whole_rows, row_start, local_rows, 0))
        solved = lax.dynamic_update_slice_in_dim(solved, whole_rows, row_block * block_rows, 0)
    return jnp.stack(pieces)


def solution(mesh):
    in_specs = (
        P(None, "prow", None),
        P(None, "prow", "pcol"),
        P("pcol", None),
        P(None, "prow", "pcol"),
        P(None, "prow", None),
    )
    out_specs = P(None, "prow", None)
    return jax.shard_map(local, mesh=mesh, in_specs=in_specs, out_specs=out_specs, check_vma=False)
```

profile of v0, /device:TPU:0, one launch (start us, length us, event | category | flops | bytes accessed | tf_op | source)
XLA Modules:
  0.0 249.5 jit_solution(15784132453054589347)
XLA Ops:
  6.5 0.7 all-gather.3.cloned.1.call-update
  7.3 10.3 %fusion.4 = f32[64,128]{1,0:T(8,128)} fusion(f32[16128,128]{1,0:T(8,128)} %param.7, f32[8,64,16128]{2,1,0:T(8,128)} %param.6), kind=kOutput, calls=%fused_computation.4 | convolution fusion | flops 1585446912 | bytes 12419072 | tf_op jit(solution)/shard_map/dot_general | solution.py:22
  17.7 8.1 %fusion.6 = f32[64,128]{1,0:T(8,128)} fusion(f32[16128,128]{1,0:T(8,128)S(1)} %copy-done, f32[8,64,16128]{2,1,0:T(8,128)} %param.6), kind=kOutput, calls=%fused_computation.6 | convolution fusion | flops 1585446912 | bytes 12419072 | tf_op jit(solution)/shard_map/dot_general | solution.py:22
  25.8 7.9 %fusion.8 = f32[64,128]{1,0:T(8,128)} fusion(f32[16128,128]{1,0:T(8,128)S(1)} %copy-done, f32[8,64,16128]{2,1,0:T(8,128)} %param.6), kind=kOutput, calls=%fused_computation.8 | convolution fusion | flops 1585446912 | bytes 12419072 | tf_op jit(solution)/shard_map/dot_general | solution.py:22
  33.7 8.1 %fusion.10 = f32[64,128]{1,0:T(8,128)} fusion(f32[16128,128]{1,0:T(8,128)S(1)} %copy-done, f32[8,64,16128]{2,1,0:T(8,128)} %param.6), kind=kOutput, calls=%fused_computation.10 | convolution fusion | flops 1585446912 | bytes 12419072 | tf_op jit(solution)/shard_map/dot_general | solution.py:22
  41.8 7.9 %fusion.12 = f32[64,128]{1,0:T(8,128)} fusion(f32[16128,128]{1,0:T(8,128)S(1)} %copy-done, f32[8,64,16128]{2,1,0:T(8,128)} %param.6), kind=kOutput, calls=%fused_computation.12 | convolution fusion | flops 1585446912 | bytes 12419072 | tf_op jit(solution)/shard_map/dot_general | solution.py:22
  49.7 8.4 %fusion.14 = f32[64,128]{1,0:T(8,128)} fusion(f32[16128,128]{1,0:T(8,128)S(1)} %copy-done, f32[8,64,16128]{2,1,0:T(8,128)} %param.6), kind=kOutput, calls=%fused_computation.14 | convolution fusion | flops 1585446912 | bytes 12419072 | tf_op jit(solution)/shard_map/dot_general | solution.py:22
  58.1 7.9 %fusion = f32[64,128]{1,0:T(8,128)} fusion(f32[16128,128]{1,0:T(8,128)S(1)} %copy-done, f32[8,64,16128]{2,1,0:T(8,128)} %param.6), kind=kOutput, calls=%fused_computation | convolution fusion | flops 1585446912 | bytes 12419072 | tf_op jit(solution)/shard_map/dot_general | solution.py:22
  66.1 8.2 %fusion.2 = f32[64,128]{1,0:T(8,128)} fusion(f32[16128,128]{1,0:T(8,128)S(1)} %copy-done, f32[8,64,16128]{2,1,0:T(8,128)} %param.6), kind=kOutput, calls=%fused_computation.2 | convolution fusion | flops 1585446912 | bytes 12419072 | tf_op jit(solution)/shard_map/dot_general | solution.py:22
  74.3 0.7 all-gather.5.cloned.1.call-update
  75.0 12.2 %all-gather.3.cloned.1.call-done = f32[8,64,2048]{2,1,0:T(8,128)} async-done(((f32[8,64,256]{2,1,0:T(8,128)}), f32[8,64,2048]{2,1,0:T(8,128)}) %all-gather.3.cloned.1.call-update) | async-done | bytes 4194320 | tf_op jit(solution)/shard_map/all_gather | solution.py:17
  87.1 1.2 fusion.38
  88.3 73.8 %all-reduce.4.cloned.1.call-done = (f32[64,128]{1,0:T(8,128)}, f32[64,128]{1,0:T(8,128)}, f32[64,128]{1,0:T(8,128)}, f32[64,128]{1,0:T(8,128)}, f32[64,128]{1,0:...) async-done(((f32[64,128]{1,0:T(8,128)}, f32[64,128]{1,0:T(8,128)}, f32[64,128]{1,0:T(8,128)}, f32[64,128]{1,0:T(8,128)}, f32[64,128]{1,0:T(8,128)}, ...) | async-done | bytes 262160 | tf_op jit(solution)/shard_map/psum | solution.py:28
  162.1 0.8 bitcast_subtract_fusion
  163.0 5.4 %all_gather.31 = f32[256,128]{1,0:T(8,128)S(1)} all-gather(f32[64,128]{1,0:T(8,128)S(1)} %bitcast_subtract_fusion), channel_id=1, replica_groups=mesh['prow'=4,'pcol'=8] {'prow'}, dimensions={0}, use_global_device_ids=true | all-gather | bytes 163840 | tf_op jit(solution)/shard_map/all_gather | solution.py:30
  168.4 17.4 %all-gather.5.cloned.1.call-done = f32[8,256,256]{2,1,0:T(8,128)} async-done(((f32[8,64,256]{2,1,0:T(8,128)}), f32[8,256,256]{2,1,0:T(8,128)}) %all-gather.5.cloned.1.call-update) | async-done | bytes 2097168 | tf_op jit(solution)/shard_map/all_gather | solution.py:16
  185.8 1.5 fusion.47
  187.3 2.1 fusion.25
  189.4 5.4 %all_gather.33 = f32[256,128]{1,0:T(8,128)S(1)} all-gather(f32[64,128]{1,0:T(8,128)S(1)} %fusion.25), channel_id=1, replica_groups=mesh['prow'=4,'pcol'=8] {'prow'}, dimensions={0}, use_global_device_ids=true | all-gather | bytes 163840 | tf_op jit(solution)/shard_map/all_gather | solution.py:30
  194.8 0.1 bitcast_dynamic-update-slice_fusion.13
  194.9 0.1 dynamic_update_slice.21
  195.0 1.4 bitcast_dynamic-update-slice_fusion.5
  196.4 2.3 fusion.27
  198.7 5.4 %all_gather.34 = f32[256,128]{1,0:T(8,128)S(1)} all-gather(f32[64,128]{1,0:T(8,128)S(1)} %fusion.27), channel_id=1, replica_groups=mesh['prow'=4,'pcol'=8] {'prow'}, dimensions={0}, use_global_device_ids=true | all-gather | bytes 163840 | tf_op jit(solution)/shard_map/all_gather | solution.py:30
  204.1 1.4 bitcast_dynamic-update-slice_fusion.4
  205.5 1.2 fusion.29
  206.7 5.6 %all_gather.35 = f32[256,128]{1,0:T(8,128)S(1)} all-gather(f32[64,128]{1,0:T(8,128)S(1)} %fusion.29), channel_id=1, replica_groups=mesh['prow'=4,'pcol'=8] {'prow'}, dimensions={0}, use_global_device_ids=true | all-gather | bytes 163840 | tf_op jit(solution)/shard_map/all_gather | solution.py:30
  212.3 0.4 bitcast_dynamic-update-slice_fusion.3
  212.7 1.2 fusion.31
  213.9 5.4 %all_gather.36 = f32[256,128]{1,0:T(8,128)S(1)} all-gather(f32[64,128]{1,0:T(8,128)S(1)} %fusion.31), channel_id=1, replica_groups=mesh['prow'=4,'pcol'=8] {'prow'}, dimensions={0}, use_global_device_ids=true | all-gather | bytes 163840 | tf_op jit(solution)/shard_map/all_gather | solution.py:30
  219.4 0.4 bitcast_dynamic-update-slice_fusion.2
  219.8 1.2 fusion.33
  221.0 5.4 %all_gather.37 = f32[256,128]{1,0:T(8,128)S(1)} all-gather(f32[64,128]{1,0:T(8,128)S(1)} %fusion.33), channel_id=1, replica_groups=mesh['prow'=4,'pcol'=8] {'prow'}, dimensions={0}, use_global_device_ids=true | all-gather | bytes 163840 | tf_op jit(solution)/shard_map/all_gather | solution.py:30
  226.4 0.4 bitcast_dynamic-update-slice_fusion.1
  226.9 1.2 fusion.35
  228.1 5.6 %all_gather.38 = f32[256,128]{1,0:T(8,128)S(1)} all-gather(f32[64,128]{1,0:T(8,128)S(1)} %fusion.35), channel_id=1, replica_groups=mesh['prow'=4,'pcol'=8] {'prow'}, dimensions={0}, use_global_device_ids=true | all-gather | bytes 163840 | tf_op jit(solution)/shard_map/all_gather | solution.py:30
  233.7 0.4 bitcast_dynamic-update-slice_fusion
  234.2 1.2 fusion.37
  235.4 5.4 %all_gather.39 = f32[256,128]{1,0:T(8,128)S(1)} all-gather(f32[64,128]{1,0:T(8,128)S(1)} %fusion.37), channel_id=1, replica_groups=mesh['prow'=4,'pcol'=8] {'prow'}, dimensions={0}, use_global_device_ids=true | all-gather | bytes 163840 | tf_op jit(solution)/shard_map/all_gather | solution.py:30
  240.8 0.1 bitcast_dynamic-update-slice_fusion.12
  240.9 0.1 bitcast_dynamic-update-slice_fusion.11
  241.0 0.1 bitcast_dynamic-update-slice_fusion.10
  241.1 0.1 bitcast_dynamic-update-slice_fusion.9
  241.2 0.1 bitcast_dynamic-update-slice_fusion.8
  241.2 0.1 bitcast_dynamic-update-slice_fusion.7
  241.3 0.4 fusion.40
  241.7 0.1 bitcast_dynamic-update-slice_fusion.6
  241.8 0.9 copy.7
  (22 shorter events, 0.1 us)
Async XLA Ops:
  6.5 80.6 %all-gather.3.cloned.1.call-start = ((), (), s32[]{:S(2)}) async-start(), calls=%async_computation | async-start | bytes 4718592 | tf_op jit(solution)/shard_map/all_gather | solution.py:17
  7.3 154.9 %all-reduce.4.cloned.1.call-start = ((), (), s32[]{:S(2)}) async-start(), calls=%async_computation.2 | async-start | bytes 524288 | tf_op jit(solution)/shard_map/psum | solution.py:28
  7.3 10.4 %copy-start = (f32[16128,128]{1,0:T(8,128)S(1)}, f32[16128,128]{1,0:T(8,128)}, u32[]{:S(2)}) copy-start(f32[16128,128]{1,0:T(8,128)} %param.7) | copy-start | bytes 24772612
  66.1 96.1 %copy-start.3 = (f32[8,64,128]{2,1,0:T(8,128)S(1)}, f32[8,64,128]{2,1,0:T(8,128)}, u32[]{:S(2)}) copy-start(f32[8,64,128]{2,1,0:T(8,128)} %param.5) | copy-start | bytes 786436
  74.2 111.6 %all-gather.5.cloned.1.call-start = ((), (), s32[]{:S(2)}) async-start(), calls=%async_computation.1 | async-start | bytes 2621440 | tf_op jit(solution)/shard_map/all_gather | solution.py:16
  162.1 43.4 %copy-start.8 = (f32[64,128]{1,0:T(8,128)S(1)}, f32[64,128]{1,0:T(8,128)}, u32[]{:S(2)}) copy-start(f32[64,128]{1,0:T(8,128)} %get-tuple-element.8) | copy-start | bytes 98308
  168.4 44.3 %copy-start.7 = (f32[64,128]{1,0:T(8,128)S(1)}, f32[64,128]{1,0:T(8,128)}, u32[]{:S(2)}) copy-start(f32[64,128]{1,0:T(8,128)} %get-tuple-element.9) | copy-start | bytes 98308
  185.8 19.7 %copy-start.1 = (f32[8,64,2048]{2,1,0:T(8,128)S(1)}, f32[8,64,2048]{2,1,0:T(8,128)}, u32[]{:S(2)}) copy-start(f32[8,64,2048]{2,1,0:T(8,128)} %all-gather.3.cloned.1.call-done) | copy-start | bytes 12582916
  185.8 26.5 %copy-start.2 = (f32[8,256,256]{2,1,0:T(8,128)S(1)}, f32[8,256,256]{2,1,0:T(8,128)}, u32[]{:S(2)}) copy-start(f32[8,256,256]{2,1,0:T(8,128)} %all-gather.5.cloned.1.call-done) | copy-start | bytes 6291460
  195.0 24.8 %copy-start.6 = (f32[64,128]{1,0:T(8,128)S(1)}, f32[64,128]{1,0:T(8,128)}, u32[]{:S(2)}) copy-start(f32[64,128]{1,0:T(8,128)} %get-tuple-element.10) | copy-start | bytes 98308
  198.7 28.2 %copy-start.5 = (f32[64,128]{1,0:T(8,128)S(1)}, f32[64,128]{1,0:T(8,128)}, u32[]{:S(2)}) copy-start(f32[64,128]{1,0:T(8,128)} %get-tuple-element.11) | copy-start | bytes 98308
  206.7 27.4 %copy-start.4 = (f32[64,128]{1,0:T(8,128)S(1)}, f32[64,128]{1,0:T(8,128)}, u32[]{:S(2)}) copy-start(f32[64,128]{1,0:T(8,128)} %get-tuple-element.12) | copy-start | bytes 98308
Sparse Core Ops, SparseCore 0:
  9.4 77.7 all-gather.2
  91.4 70.6 all-reduce.3
  163.8 21.9 all-gather.4
where the time goes:
time: 253 us; the launch traced here: 249 us
  waiting for transfers between devices  105 us (42%)
  matrix products  83.6 us (33%)
  blocking collectives  43.7 us (17%)
  between operations  13.6 us (5%)
    psum x1, waiting for transfers between devices, local(): earlier_here = lax.psum(earlier_part, 'pcol')  73.8 us
    dot_general x8, matrix products, local(): jnp.dot(lower_prev[row_block], solved_prev, precision=highest, preferred_...  66.9 us
    all_gather x8, blocking collectives, local(): residual = lax.all_gather(local_residual, 'prow', axis=0, tiled=True)  43.7 us
    all_gather x1, waiting for transfers between devices, local(): full_inverse = lax.all_gather(inverse_diag, 'prow', axis=1, tiled=True)  17.4 us
    all_gather x1, waiting for transfers between devices, local(): full_window = lax.all_gather(lower_window, 'pcol', axis=2, tiled=True)  12.2 us
    dot_general x7, matrix products, local(): jnp.dot(full_window[row_block], solved, precision=highest, preferred_elem...  10.4 us
    dot_general x8, matrix products, local(): jnp.dot(full_inverse[row_block], residual, precision=highest, preferred_e...  6.33 us
  transfers between devices with their start and end apart: 3, of which 3 were waited for; matrix products, arithmetic and copies ran while one was open for 28% of the time, Pallas kernels for 0%

commit v1 on v0

--- a/solution.py
+++ b/solution.py
@@ -25,7 +25,8 @@
             precision=highest,
             preferred_element_type=jnp.float32,
         )
-        earlier_here = lax.psum(earlier_part, "pcol")
+        parts = lax.all_gather(earlier_part, "pcol", axis=0, tiled=False)
+        earlier_here = parts.sum(axis=0)
         local_residual = right_side[row_block] - (earlier_here + window_term)
         residual = lax.all_gather(local_residual, "prow", axis=0, tiled=True)
         whole_rows = jnp.dot(

time: 253 us -> 398 us (1.57)
  blocking collectives: 43.7 us -> 294 us
  waiting for transfers between devices: 105 us -> 1.43 us
    all_gather x0 -> x8, blocking collectives: none -> 250 us  [local(): parts = lax.all_gather(earlier_part, 'pcol', axis=0, tiled=False)]
    psum x1 -> x0, waiting for transfers between devices: 73.8 us -> none  [local(): earlier_here = lax.psum(earlier_part, 'pcol')]
    all_gather x1, waiting for transfers between devices: 17.4 us -> 0.01 us  [local(): full_inverse = lax.all_gather(inverse_diag, 'prow', axis=1, tiled=True)]
    all_gather x1, waiting for transfers between devices: 12.2 us -> 0.02 us  [local(): full_window = lax.all_gather(lower_window, 'pcol', axis=2, tiled=True)]
  transfers between devices with their start and end apart: 3 -> 2, of which waited for: 3 -> 0; matrix products, arithmetic and copies ran while one was open for 28% -> 17% of each run, Pallas kernels for 0% -> 0%
where the time goes in v1:
time: 398 us; the launch traced here: 395 us
  blocking collectives  294 us (74%)
  matrix products  82.5 us (21%)
  between operations  13.9 us (3%)
    all_gather x8, blocking collectives, local(): parts = lax.all_gather(earlier_part, 'pcol', axis=0, tiled=False)  250 us
    dot_general x8, matrix products, local(): jnp.dot(lower_prev[row_block], solved_prev, precision=highest, preferred_...  66 us
    all_gather x8, blocking collectives, local(): residual = lax.all_gather(local_residual, 'prow', axis=0, tiled=True)  43.6 us
    dot_general x7, matrix products, local(): jnp.dot(full_window[row_block], solved, precision=highest, preferred_elem...  10.2 us
  transfers between devices with their start and end apart: 2, of which 0 were waited for; matrix products, arithmetic and copies ran while one was open for 17% of the time, Pallas kernels for 0%

profile of v1, /device:TPU:0, one launch (start us, length us, event | category | flops | bytes accessed | tf_op | source)
XLA Modules:
  0.0 394.9 jit_solution(330838243085122896)
XLA Ops:
  6.5 0.7 all-gather.11.cloned.1.call-update
  7.3 0.7 all-gather.13.cloned.1.call-update
  8.0 10.4 %fusion.14 = f32[64,128]{1,0:T(8,128)S(1)} fusion(f32[16128,128]{1,0:T(8,128)} %param.7, f32[8,64,16128]{2,1,0:T(8,128)} %param.6), kind=kOutput, calls=%fused_computation.14 | convolution fusion | flops 1585446912 | bytes 12419072 | tf_op jit(solution)/shard_map/dot_general | solution.py:22
  18.4 7.6 %fusion.12 = f32[64,128]{1,0:T(8,128)S(1)} fusion(f32[16128,128]{1,0:T(8,128)S(1)} %copy-done, f32[8,64,16128]{2,1,0:T(8,128)} %param.6), kind=kOutput, calls=%fused_computation.12 | convolution fusion | flops 1585446912 | bytes 12419072 | tf_op jit(solution)/shard_map/dot_general | solution.py:22
  26.0 7.3 %fusion.10 = f32[64,128]{1,0:T(8,128)S(1)} fusion(f32[16128,128]{1,0:T(8,128)S(1)} %copy-done, f32[8,64,16128]{2,1,0:T(8,128)} %param.6), kind=kOutput, calls=%fused_computation.10 | convolution fusion | flops 1585446912 | bytes 12419072 | tf_op jit(solution)/shard_map/dot_general | solution.py:22
  33.3 7.5 %fusion.8 = f32[64,128]{1,0:T(8,128)S(1)} fusion(f32[16128,128]{1,0:T(8,128)S(1)} %copy-done, f32[8,64,16128]{2,1,0:T(8,128)} %param.6), kind=kOutput, calls=%fused_computation.8 | convolution fusion | flops 1585446912 | bytes 12419072 | tf_op jit(solution)/shard_map/dot_general | solution.py:22
  40.8 33.7 %all-gather = f32[512,128]{1,0:T(8,128)S(1)} all-gather(f32[64,128]{1,0:T(8,128)S(1)} %fusion.14), channel_id=2, replica_groups=mesh['prow'=4,'pcol'=8] {'pcol'}, dimensions={0}, use_global_device_ids=true | all-gather | bytes 294912 | tf_op jit(solution)/shard_map/all_gather | solution.py:28
  74.5 31.7 %all-gather.1 = f32[512,128]{1,0:T(8,128)S(1)} all-gather(f32[64,128]{1,0:T(8,128)S(1)} %fusion.12), channel_id=3, replica_groups=mesh['prow'=4,'pcol'=8] {'pcol'}, dimensions={0}, use_global_device_ids=true | all-gather | bytes 294912 | tf_op jit(solution)/shard_map/all_gather | solution.py:28
  106.3 30.9 %all-gather.2 = f32[512,128]{1,0:T(8,128)S(1)} all-gather(f32[64,128]{1,0:T(8,128)S(1)} %fusion.10), channel_id=4, replica_groups=mesh['prow'=4,'pcol'=8] {'pcol'}, dimensions={0}, use_global_device_ids=true | all-gather | bytes 294912 | tf_op jit(solution)/shard_map/all_gather | solution.py:28
  137.2 30.8 %all-gather.3 = f32[512,128]{1,0:T(8,128)S(1)} all-gather(f32[64,128]{1,0:T(8,128)S(1)} %fusion.8), channel_id=5, replica_groups=mesh['prow'=4,'pcol'=8] {'pcol'}, dimensions={0}, use_global_device_ids=true | all-gather | bytes 294912 | tf_op jit(solution)/shard_map/all_gather | solution.py:28
  168.0 8.2 %fusion.6 = f32[64,128]{1,0:T(8,128)S(1)} fusion(f32[16128,128]{1,0:T(8,128)} %param.7, f32[8,64,16128]{2,1,0:T(8,128)} %param.6), kind=kOutput, calls=%fused_computation.6 | convolution fusion | flops 1585446912 | bytes 12419072 | tf_op jit(solution)/shard_map/dot_general | solution.py:22
  176.3 30.8 %all-gather.4 = f32[512,128]{1,0:T(8,128)S(1)} all-gather(f32[64,128]{1,0:T(8,128)S(1)} %fusion.6), channel_id=6, replica_groups=mesh['prow'=4,'pcol'=8] {'pcol'}, dimensions={0}, use_global_device_ids=true | all-gather | bytes 294912 | tf_op jit(solution)/shard_map/all_gather | solution.py:28
  207.1 8.2 %fusion.4 = f32[64,128]{1,0:T(8,128)S(1)} fusion(f32[16128,128]{1,0:T(8,128)} %param.7, f32[8,64,16128]{2,1,0:T(8,128)} %param.6), kind=kOutput, calls=%fused_computation.4 | convolution fusion | flops 1585446912 | bytes 12419072 | tf_op jit(solution)/shard_map/dot_general | solution.py:22
  215.4 30.9 %all-gather.5 = f32[512,128]{1,0:T(8,128)S(1)} all-gather(f32[64,128]{1,0:T(8,128)S(1)} %fusion.4), channel_id=7, replica_groups=mesh['prow'=4,'pcol'=8] {'pcol'}, dimensions={0}, use_global_device_ids=true | all-gather | bytes 294912 | tf_op jit(solution)/shard_map/all_gather | solution.py:28
  246.3 8.5 %fusion.2 = f32[64,128]{1,0:T(8,128)S(1)} fusion(f32[16128,128]{1,0:T(8,128)} %param.7, f32[8,64,16128]{2,1,0:T(8,128)} %param.6), kind=kOutput, calls=%fused_computation.2 | convolution fusion | flops 1585446912 | bytes 12419072 | tf_op jit(solution)/shard_map/dot_general | solution.py:22
  254.7 30.8 %all-gather.6 = f32[512,128]{1,0:T(8,128)S(1)} all-gather(f32[64,128]{1,0:T(8,128)S(1)} %fusion.2), channel_id=8, replica_groups=mesh['prow'=4,'pcol'=8] {'pcol'}, dimensions={0}, use_global_device_ids=true | all-gather | bytes 294912 | tf_op jit(solution)/shard_map/all_gather | solution.py:28
  285.5 8.3 %fusion = f32[64,128]{1,0:T(8,128)S(1)} fusion(f32[16128,128]{1,0:T(8,128)} %param.7, f32[8,64,16128]{2,1,0:T(8,128)} %param.6), kind=kOutput, calls=%fused_computation | convolution fusion | flops 1585446912 | bytes 12419072 | tf_op jit(solution)/shard_map/dot_general | solution.py:22
  293.8 30.7 %all-gather.7 = f32[512,128]{1,0:T(8,128)S(1)} all-gather(f32[64,128]{1,0:T(8,128)S(1)} %fusion), channel_id=9, replica_groups=mesh['prow'=4,'pcol'=8] {'pcol'}, dimensions={0}, use_global_device_ids=true | all-gather | bytes 294912 | tf_op jit(solution)/shard_map/all_gather | solution.py:28
  324.6 1.2 fusion.38
  325.9 5.4 %all_gather.81 = f32[256,128]{1,0:T(8,128)S(1)} all-gather(f32[64,128]{1,0:T(8,128)S(1)} %bitcast_subtract_fusion), channel_id=1, replica_groups=mesh['prow'=4,'pcol'=8] {'prow'}, dimensions={0}, use_global_device_ids=true | all-gather | bytes 163840 | tf_op jit(solution)/shard_map/all_gather | solution.py:31
  331.3 1.5 fusion.47
  332.8 0.1 bitcast_dynamic-update-slice_fusion.13
  332.9 0.1 dynamic_update_slice.21
  333.0 1.9 fusion.25
  334.9 5.4 %all_gather.85 = f32[256,128]{1,0:T(8,128)S(1)} all-gather(f32[64,128]{1,0:T(8,128)S(1)} %fusion.25), channel_id=1, replica_groups=mesh['prow'=4,'pcol'=8] {'prow'}, dimensions={0}, use_global_device_ids=true | all-gather | bytes 163840 | tf_op jit(solution)/shard_map/all_gather | solution.py:31
  340.3 1.4 bitcast_dynamic-update-slice_fusion.5
  341.7 2.2 fusion.27
  343.9 5.4 %all_gather.88 = f32[256,128]{1,0:T(8,128)S(1)} all-gather(f32[64,128]{1,0:T(8,128)S(1)} %fusion.27), channel_id=1, replica_groups=mesh['prow'=4,'pcol'=8] {'prow'}, dimensions={0}, use_global_device_ids=true | all-gather | bytes 163840 | tf_op jit(solution)/shard_map/all_gather | solution.py:31
  349.4 1.4 bitcast_dynamic-update-slice_fusion.4
  350.8 1.2 fusion.29
  352.0 5.4 %all_gather.91 = f32[256,128]{1,0:T(8,128)S(1)} all-gather(f32[64,128]{1,0:T(8,128)S(1)} %fusion.29), channel_id=1, replica_groups=mesh['prow'=4,'pcol'=8] {'prow'}, dimensions={0}, use_global_device_ids=true | all-gather | bytes 163840 | tf_op jit(solution)/shard_map/all_gather | solution.py:31
  357.4 0.4 bitcast_dynamic-update-slice_fusion.3
  357.8 1.2 fusion.31
  359.0 5.7 %all_gather.94 = f32[256,128]{1,0:T(8,128)S(1)} all-gather(f32[64,128]{1,0:T(8,128)S(1)} %fusion.31), channel_id=1, replica_groups=mesh['prow'=4,'pcol'=8] {'prow'}, dimensions={0}, use_global_device_ids=true | all-gather | bytes 163840 | tf_op jit(solution)/shard_map/all_gather | solution.py:31
  364.7 0.4 bitcast_dynamic-update-slice_fusion.2
  365.1 1.2 fusion.33
  366.3 5.4 %all_gather.97 = f32[256,128]{1,0:T(8,128)S(1)} all-gather(f32[64,128]{1,0:T(8,128)S(1)} %fusion.33), channel_id=1, replica_groups=mesh['prow'=4,'pcol'=8] {'prow'}, dimensions={0}, use_global_device_ids=true | all-gather | bytes 163840 | tf_op jit(solution)/shard_map/all_gather | solution.py:31
  371.8 0.4 bitcast_dynamic-update-slice_fusion.1
  372.2 1.2 fusion.35
  373.4 5.4 %all_gather.100 = f32[256,128]{1,0:T(8,128)S(1)} all-gather(f32[64,128]{1,0:T(8,128)S(1)} %fusion.35), channel_id=1, replica_groups=mesh['prow'=4,'pcol'=8] {'prow'}, dimensions={0}, use_global_device_ids=true | all-gather | bytes 163840 | tf_op jit(solution)/shard_map/all_gather | solution.py:31
  378.8 0.4 bitcast_dynamic-update-slice_fusion
  379.3 1.2 fusion.37
  380.5 5.4 %all_gather.103 = f32[256,128]{1,0:T(8,128)S(1)} all-gather(f32[64,128]{1,0:T(8,128)S(1)} %fusion.37), channel_id=1, replica_groups=mesh['prow'=4,'pcol'=8] {'prow'}, dimensions={0}, use_global_device_ids=true | all-gather | bytes 163840 | tf_op jit(solution)/shard_map/all_gather | solution.py:31
  386.0 0.1 bitcast_dynamic-update-slice_fusion.11
  386.2 0.1 bitcast_dynamic-update-slice_fusion.9
  386.4 0.1 bitcast_dynamic-update-slice_fusion.7
  386.4 0.4 fusion.40
  386.9 0.9 copy.7
  (25 shorter events, 0.7 us)
Async XLA Ops:
  6.5 318.1 %all-gather.11.cloned.1.call-start = ((), (), s32[]{:S(2)}) async-start(), calls=%async_computation | async-start | bytes 4718592 | tf_op jit(solution)/shard_map/all_gather | solution.py:17
  7.3 324.0 %all-gather.13.cloned.1.call-start = ((), (), s32[]{:S(2)}) async-start(), calls=%async_computation.1 | async-start | bytes 2621440 | tf_op jit(solution)/shard_map/all_gather | solution.py:16
  8.0 10.4 %copy-start = (f32[16128,128]{1,0:T(8,128)S(1)}, f32[16128,128]{1,0:T(8,128)}, u32[]{:S(2)}) copy-start(f32[16128,128]{1,0:T(8,128)} %param.7) | copy-start | bytes 24772612
  285.5 40.3 %copy-start.3 = (f32[8,64,128]{2,1,0:T(8,128)S(1)}, f32[8,64,128]{2,1,0:T(8,128)}, u32[]{:S(2)}) copy-start(f32[8,64,128]{2,1,0:T(8,128)} %param.5) | copy-start | bytes 786436
  331.3 19.5 %copy-start.1 = (f32[8,64,2048]{2,1,0:T(8,128)S(1)}, f32[8,64,2048]{2,1,0:T(8,128)}, u32[]{:S(2)}) copy-start(f32[8,64,2048]{2,1,0:T(8,128)} %all-gather.11.cloned.1.call-done) | copy-start | bytes 12582916
  331.3 26.1 %copy-start.2 = (f32[8,256,256]{2,1,0:T(8,128)S(1)}, f32[8,256,256]{2,1,0:T(8,128)}, u32[]{:S(2)}) copy-start(f32[8,256,256]{2,1,0:T(8,128)} %all-gather.13.cloned.1.call-done) | copy-start | bytes 6291460
Sparse Core Ops, SparseCore 0:
  9.4 83.2 all-gather.10
  94.3 21.2 all-gather.12
